TPU v7x, 256 devices: a whole 4x4x8 slice. The times are simulated.
256 devices in a mesh: gx: 8 (over x, core), gy: 4 (over z_lo), gz: 8 (over y, z_hi).
Axes of the slice: x: 4, y: 4, z: 8 (z_hi: 2, z_lo: 4; z = z_hi * 4 + z_lo), core: 2. Of those that a mesh axis runs over, the one named last changes fastest.
Arguments:
- start_block: float32 [32, 3, 2, 8, 16, 1024], P(None, None, None, 'gx', 'gy', 'gz'), may hold values from -700 to 700
- pair_blocks: float32 [3, 3, 16, 2, 8, 16, 1024], P(None, None, None, None, 'gx', 'gy', 'gz'), may hold values from -8 to 8, as said below
- slot_map: int32 [16, 2, 8, 16, 1024], P(None, None, 'gx', 'gy', 'gz'), may hold values from 0 to 15, as said below
Outputs:
- alpha1: float32 [32, 32], replicated
- alpha2: float32 [32, 32], replicated
- beta1: float32 [32, 32], replicated
- beta2: float32 [32, 32], replicated
- basis3: float32 [32, 3, 2, 8, 16, 1024], P(None, None, None, 'gx', 'gy', 'gz')
Inputs may be any that keep to these rules, and one draw needn't show every extreme that they name: `slot_map`: for every atom the 16 slots hold each of 0 to 15 once; 0 to 13 name the neighbour directions of the steps, 14 and 15 mark padding slots. `pair_blocks`: the block an atom holds toward a neighbour is the transpose of the block that neighbour holds toward the atom, so H is symmetric.
All inputs are finite; a program needn't handle non-finite values.
Results may differ from a plain program's by a relative error of at most 0.0003.
Values sent between devices are 32-bit elements; how exact they have to be, the bound alone decides.
A program may use at most 64 MiB of HBM per device.

v0:
```python
import jax
import jax.numpy as jnp
from jax import lax
from jax.sharding import PartitionSpec as P

PRECISE = lax.Precision.HIGHEST


def extended(block, sides, width):
    for axis, dim in sides:
        count = lax.axis_size(axis)
        forward = [(i, i + 1) for i in range(count - 1)]
        forward.append((count - 1, 0))
        backward = [(target, source) for source, target in forward]
        low = lax.ppermute(
            lax.slice_in_dim(block, block.shape[dim] - width, None, axis=dim), axis, forward
        )
        high = lax.ppermute(lax.slice_in_dim(block, 0, width, axis=dim), axis, backward)
        block = jnp.concatenate([low, block, high], axis=dim)
    return block


def neighbour_offset(sublattice, offset_id):
    if offset_id < 8:
        corner_bits = (offset_id >> 2 & 1, offset_id >> 1 & 1, offset_id & 1)
        if sublattice == 0:
            return ((-corner_bits[0], -corner_bits[1], -corner_bits[2]), 1)
        return (corner_bits, 0)
    axis_id = (offset_id - 8) // 2
    direction = 1 if (offset_id - 8) % 2 == 0 else -1
    displacement = tuple((direction if axis_number == axis_id else 0 for axis_number in range(3)))
    return (displacement, sublattice)


def offset_blocks(pair_blocks, slot_map):
    result = []
    for offset_id in range(14):
        chosen = slot_map[None, None] == offset_id
        result.append(jnp.sum(jnp.where(chosen, pair_blocks, jnp.float32(0.0)), axis=2))
    return result


def onsite_blocks(blocks):
    result = []
    for sublattice in range(2):
        onsite = jnp.zeros(blocks[0].shape[:2] + blocks[0].shape[3:], jnp.float32)
        for offset_id in range(14):
            coupling = blocks[offset_id][:, :, sublattice]
            onsite = onsite + 0.5 * (coupling + jnp.swapaxes(coupling, 0, 1))
        result.append(onsite)
    return result


def apply_hessian(vectors, blocks, onsite):
    padded = extended(vectors, (("gx", 3), ("gy", 4), ("gz", 5)), 1)
    size_x, size_y, size_z = (vectors.shape[3], vectors.shape[4], vectors.shape[5])
    outputs = []
    for sublattice in range(2):
        summed = jnp.zeros(vectors.shape[:2] + vectors.shape[3:], jnp.float32)
        for offset_id in range(14):
            displacement, source = neighbour_offset(sublattice, offset_id)
            start_x = 1 + displacement[0]
            start_y = 1 + displacement[1]
            start_z = 1 + displacement[2]
            neighbour = padded[
                :,
                :,
                source,
                start_x : start_x + size_x,
                start_y : start_y + size_y,
                start_z : start_z + size_z,
            ]
            coupling = blocks[offset_id][:, :, sublattice]
            summed = summed + jnp.sum(coupling[None] * neighbour[:, None], axis=2)
        summed = summed - jnp.sum(
            onsite[sublattice][None] * vectors[:, None, :, sublattice], axis=2
        )
        outputs.append(summed)
    return jnp.stack(outputs, axis=2)


def local_gram(left, right):
    left_flat = left.reshape(left.shape[0], -1)
    right_flat = right.reshape(right.shape[0], -1)
    return lax.dot_general(left_flat, right_flat, (((1,), (1,)), ((), ())), precision=PRECISE)


def combine(matrix, vectors):
    flat = vectors.reshape(vectors.shape[0], -1)
    return jnp.dot(matrix, flat, precision=PRECISE).reshape(vectors.shape)


def inverse_factor(gram_matrix):
    lower = jnp.linalg.cholesky(gram_matrix)
    identity = jnp.eye(gram_matrix.shape[0], dtype=gram_matrix.dtype)
    inverse = jax.scipy.linalg.solve_triangular(lower, identity, lower=True)
    return (lower, inverse)


def lanczos_step(basis, image, previous, coupling_prev, row_count):
    alpha = lax.psum(local_gram(image, basis), ("gx", "gy", "gz")) / row_count
    residual = image - combine(alpha, basis)
    if previous is not None:
        residual = residual - combine(coupling_prev.T, previous)
    residual_gram = lax.psum(local_gram(residual, residual), ("gx", "gy", "gz")) / row_count
    return (alpha, residual, residual_gram)


def local(start_block, pair_blocks, slot_map):
    device_count = lax.axis_size("gx") * lax.axis_size("gy") * lax.axis_size("gz")
    row_count = start_block[0].size * device_count
    blocks = offset_blocks(pair_blocks, slot_map)
    onsite = onsite_blocks(blocks)
    start_gram = lax.psum(local_gram(start_block, start_block), ("gx", "gy", "gz")) / row_count
    lower0, inverse0 = inverse_factor(start_gram)
    basis1 = combine(inverse0, start_block)
    image1 = apply_hessian(basis1, blocks, onsite)
    alpha1, residual1, gram_first = lanczos_step(basis1, image1, None, None, row_count)
    beta1, inverse1 = inverse_factor(gram_first)
    basis2 = combine(inverse1, residual1)
    image2 = apply_hessian(basis2, blocks, onsite)
    alpha2, residual2, gram_second = lanczos_step(basis2, image2, basis1, beta1, row_count)
    beta2, inverse2 = inverse_factor(gram_second)
    basis3 = combine(inverse2, residual2)
    return (alpha1, alpha2, beta1, beta2, basis3)


def solution(mesh):
    in_specs = (
        P(None, None, None, "gx", "gy", "gz"),
        P(None, None, None, None, "gx", "gy", "gz"),
        P(None, None, "gx", "gy", "gz"),
    )
    out_specs = (P(), P(), P(), P(), P(None, None, None, "gx", "gy", "gz"))
    return jax.shard_map(local, mesh=mesh, in_specs=in_specs, out_specs=out_specs, check_vma=False)
```

profile of v0, /device:TPU:1, one launch (start us, length us, event | category | flops | bytes accessed | tf_op | source)
XLA Modules:
  0.0 522.5 jit_solution(3226206658296597986)
XLA Ops:
  0.6 1.2 reshape.1549
  1.8 1.6 convolution_bitcast_fusion.2
  3.4 81.5 %psum.35 = f32[32,32]{0,1:T(8,128)S(1)} all-reduce(f32[32,32]{0,1:T(8,128)S(1)} %convolution_bitcast_fusion.2), channel_id=1, replica_groups=mesh['gx'=8,'gy'=4,'gz'=8] {'gx','gy','gz'}, use_global_device_ids=true, to_apply=%region_1.2 | all-reduce | flops 1024 | bytes 8192 | tf_op jit(solution)/shard_map/psum | solution.py:114
  85.0 2.9 cholesky.59
  88.6 0.7 fusion.44
  89.3 2.4 custom-call.7
  92.8 1.0 collective-permute-start.1
  94.1 2.5 select_reduce_fusion.13
  103.9 0.8 multiply_reduce_fusion.45
  104.7 0.8 multiply_reduce_fusion.59
  106.4 2.7 collective-permute-start.3
  109.2 0.7 slice_bitcast_fusion.9
  109.9 0.7 multiply_reduce_fusion.50
  110.6 0.9 multiply_reduce_fusion.55
  111.5 0.9 multiply_reduce_fusion.51
  112.3 1.1 collective-permute-done.2
  113.4 6.9 %collective-permute-done.3 = f32[32,3,2,3,1,128]{5,0,4,3,2,1:T(8,128)S(1)} collective-permute-done((f32[32,3,2,3,1,128]{5,0,4,3,2,1:T(8,128)S(1)}, f32[32,3,2,3,1,128]{5,0,4,3,2,1:T(8,128)S(1)}, u32[]{:S(2)}, u32[]{:S(2)}) %collective-permute-start.3) | collective-permute-done | bytes 294944 | tf_op jit(solution)/shard_map/ppermute | solution.py:18
  120.3 0.7 copy-done.10
  121.2 1.8 fusion.52
  123.1 2.8 copy.507
  125.9 5.6 %collective-permute-start.5 = (f32[32,3,2,3,6,1]{0,2,5,4,3,1:T(2,128)}, f32[32,3,2,3,6,1]{0,2,5,4,3,1:T(2,128)}, u32[]{:S(2)}, u32[]{:S(2)}) collective-permute-start(f32[32,3,2,3,6,1]{0,2,5,4,3,1:T(2,128)} %copy.507), channel_id=1, source_target_pairs={{1,0},{2,1},{3,2},{4,3},{5,4},{6,5},{7,6},{0,7},{9,8},{10,9},{11,1... | collective-permute-start | bytes 41480 | tf_op jit(solution)/shard_map/ppermute | solution.py:18
  131.5 1.3 copy.506
  132.8 1.7 multiply_reduce_fusion.36
  134.5 2.7 copy.419
  137.2 5.0 collective-permute-done.4
  142.2 1.5 copy.395
  143.8 1.4 fusion.8
  151.0 74.3 %psum.36 = f32[32,32]{0,1:T(8,128)S(1)} all-reduce(f32[32,32]{0,1:T(8,128)S(1)} %fusion.56), channel_id=1, replica_groups=mesh['gx'=8,'gy'=4,'gz'=8] {'gx','gy','gz'}, use_global_device_ids=true, to_apply=%region_47.50 | all-reduce | flops 1024 | bytes 8192 | tf_op jit(solution)/shard_map/psum | solution.py:101
  226.4 73.7 %psum.37 = f32[32,32]{0,1:T(8,128)S(1)} all-reduce(f32[32,32]{0,1:T(8,128)S(1)} %fusion.57), channel_id=1, replica_groups=mesh['gx'=8,'gy'=4,'gz'=8] {'gx','gy','gz'}, use_global_device_ids=true, to_apply=%region_48.51 | all-reduce | flops 1024 | bytes 8192 | tf_op jit(solution)/shard_map/psum | solution.py:105
  300.2 2.9 cholesky.70
  304.4 2.4 custom-call.8
  307.9 1.2 collective-permute-start.6
  309.2 0.8 multiply_reduce_fusion.15
  310.1 0.8 multiply_reduce_fusion.29
  311.0 0.7 copy.495
  311.7 2.2 collective-permute-done.6
  314.0 2.6 collective-permute-done.7
  316.7 1.0 collective-permute-start.8
  317.7 2.4 collective-permute-start.9
  320.2 0.7 multiply_reduce_fusion.20
  320.9 0.9 multiply_reduce_fusion.25
  321.8 0.9 multiply_reduce_fusion.21
  322.6 4.1 collective-permute-done.8
  326.7 5.3 %collective-permute-done.9 = f32[32,3,2,3,1,128]{5,0,4,3,2,1:T(8,128)S(1)} collective-permute-done((f32[32,3,2,3,1,128]{5,0,4,3,2,1:T(8,128)S(1)}, f32[32,3,2,3,1,128]{5,0,4,3,2,1:T(8,128)S(1)}, u32[]{:S(2)}, u32[]{:S(2)}) %collective-permute-start.9) | collective-permute-done | bytes 294944 | tf_op jit(solution)/shard_map/ppermute | solution.py:18
  332.0 0.7 copy-done.6
  332.9 1.8 fusion.51
  334.8 2.8 copy.509
  337.6 4.7 collective-permute-start.11
  342.2 1.5 multiply_reduce_fusion.6
  343.7 1.3 copy.508
  345.0 0.7 collective-permute-start.10
  345.7 1.5 copy.488
  347.2 2.2 maximum_bitcast_fusion.4
  349.5 0.9 multiply_reduce_fusion.17
  350.4 4.6 collective-permute-done.10
  354.9 1.5 copy.486
  356.5 1.4 fusion.4
  363.7 73.7 %psum.38 = f32[32,32]{0,1:T(8,128)S(1)} all-reduce(f32[32,32]{0,1:T(8,128)S(1)} %fusion.59), channel_id=1, replica_groups=mesh['gx'=8,'gy'=4,'gz'=8] {'gx','gy','gz'}, use_global_device_ids=true, to_apply=%region_79.82 | all-reduce | flops 1024 | bytes 8192 | tf_op jit(solution)/shard_map/psum | solution.py:101
  439.1 73.7 %psum.39 = f32[32,32]{0,1:T(8,128)S(1)} all-reduce(f32[32,32]{0,1:T(8,128)S(1)} %fusion.60), channel_id=1, replica_groups=mesh['gx'=8,'gy'=4,'gz'=8] {'gx','gy','gz'}, use_global_device_ids=true, to_apply=%region_80.83 | all-reduce | flops 1024 | bytes 8192 | tf_op jit(solution)/shard_map/psum | solution.py:105
  512.8 2.9 cholesky.81
  516.4 1.3 select_bitcast_fusion
  517.6 2.4 custom-call.9
  520.8 1.0 copy.497
  521.8 0.7 copy.496
  (321 shorter events, 28.2 us)
Async XLA Ops:
  3.4 90.4 %copy-start.95 = (s32[16,2,1,4,128]{4,3,2,1,0:T(4,128)S(1)}, s32[16,2,1,4,128]{4,3,2,1,0:T(4,128)}, u32[]{:S(2)}) copy-start(s32[16,2,1,4,128]{4,3,2,1,0:T(4,128)} %param.8) | copy-start | bytes 196612
  88.6 5.5 %copy-start.35 = (f32[3,3,16,2,1,4,128]{6,5,4,3,2,1,0:T(4,128)S(1)}, f32[3,3,16,2,1,4,128]{6,5,4,3,2,1,0:T(4,128)}, u32[]{:S(2)}) copy-start(f32[3,3,16,2,1,4,128]{6,5,4,3,2,1,0:T(4,128)} %param.7) | copy-start | bytes 1769476
  92.8 12.8 %collective-permute-start = (f32[32,3,2,1,4,128]{5,0,4,3,2,1:T(8,128)S(1)}, f32[32,3,2,1,4,128]{5,0,4,3,2,1:T(8,128)S(1)}, u32[]{:S(2)}, u32[]{:S(2)}) collective-permute-start(f32[32,3,2,1,4,128]{5,0,4,3,2,1:T(8,128)S(1)} %copy.391), channel_id=1, source_target_pairs={{0,32},{32,64},{64,96},{96,128},{128,160},{160,192},{192,224},{224... | collective-permute-start | bytes 1179656 | tf_op jit(solution)/shard_map/ppermute | solution.py:15
  92.8 12.9 %collective-permute-start.1 = (f32[32,3,2,1,4,128]{5,0,4,3,2,1:T(8,128)S(1)}, f32[32,3,2,1,4,128]{5,0,4,3,2,1:T(8,128)S(1)}, u32[]{:S(2)}, u32[]{:S(2)}) collective-permute-start(f32[32,3,2,1,4,128]{5,0,4,3,2,1:T(8,128)S(1)} %copy.391), channel_id=1, source_target_pairs={{32,0},{64,32},{96,64},{128,96},{160,128},{192,160},{224,192},{0,2... | collective-permute-start | bytes 1179656 | tf_op jit(solution)/shard_map/ppermute | solution.py:18
  99.9 10.0 %copy-start.84 = (f32[3,3,4,128]{3,2,0,1:T(4,128)}, f32[3,3,4,128]{3,2,0,1:T(4,128)S(1)}, u32[]{:S(2)}) copy-start(f32[3,3,4,128]{3,2,0,1:T(4,128)S(1)} %get-tuple-element.159) | copy-start | bytes 55300
  99.9 10.7 %copy-start.82 = (f32[3,3,4,128]{3,2,0,1:T(4,128)}, f32[3,3,4,128]{3,2,0,1:T(4,128)S(1)}, u32[]{:S(2)}) copy-start(f32[3,3,4,128]{3,2,0,1:T(4,128)S(1)} %get-tuple-element.162) | copy-start | bytes 55300
  100.5 10.9 %copy-start.80 = (f32[3,3,4,128]{3,2,0,1:T(4,128)}, f32[3,3,4,128]{3,2,0,1:T(4,128)S(1)}, u32[]{:S(2)}) copy-start(f32[3,3,4,128]{3,2,0,1:T(4,128)S(1)} %get-tuple-element.194) | copy-start | bytes 55300
  102.5 8.1 %copy-start.88 = (f32[3,3,4,128]{3,2,0,1:T(4,128)}, f32[3,3,4,128]{3,2,0,1:T(4,128)S(1)}, u32[]{:S(2)}) copy-start(f32[3,3,4,128]{3,2,0,1:T(4,128)S(1)} %get-tuple-element.190) | copy-start | bytes 55300
  102.5 9.0 %copy-start.86 = (f32[3,3,4,128]{3,2,0,1:T(4,128)}, f32[3,3,4,128]{3,2,0,1:T(4,128)S(1)}, u32[]{:S(2)}) copy-start(f32[3,3,4,128]{3,2,0,1:T(4,128)S(1)} %get-tuple-element.189) | copy-start | bytes 55300
  103.8 1.8 copy-start.90
  103.8 1.8 copy-start.92
  103.9 1.9 copy-start.36
  104.7 1.1 copy-start.38
  105.8 7.6 %collective-permute-start.2 = (f32[32,3,2,3,1,128]{5,0,4,3,2,1:T(8,128)S(1)}, f32[32,3,2,3,1,128]{5,0,4,3,2,1:T(8,128)S(1)}, u32[]{:S(2)}, u32[]{:S(2)}) collective-permute-start(f32[32,3,2,3,1,128]{5,0,4,3,2,1:T(8,128)S(1)} %get-tuple-element.115), channel_id=1, source_target_pairs={{0,8},{8,16},{16,24},{24,0},{1,9},{9,17},{17,25},{25,1},{2,10},{10... | collective-permute-start | bytes 884744 | tf_op jit(solution)/shard_map/ppermute | solution.py:15
  106.4 13.9 %collective-permute-start.3 = (f32[32,3,2,3,1,128]{5,0,4,3,2,1:T(8,128)S(1)}, f32[32,3,2,3,1,128]{5,0,4,3,2,1:T(8,128)S(1)}, u32[]{:S(2)}, u32[]{:S(2)}) collective-permute-start(f32[32,3,2,3,1,128]{5,0,4,3,2,1:T(8,128)S(1)} %get-tuple-element.116), channel_id=1, source_target_pairs={{8,0},{16,8},{24,16},{0,24},{9,1},{17,9},{25,17},{1,25},{10,2},{18... | collective-permute-start | bytes 884744 | tf_op jit(solution)/shard_map/ppermute | solution.py:18
  113.4 6.9 %copy-start.8 = (f32[32,3,2,3,1,128]{5,0,4,3,2,1:T(8,128)}, f32[32,3,2,3,1,128]{5,0,4,3,2,1:T(8,128)S(1)}, u32[]{:S(2)}) copy-start(f32[32,3,2,3,1,128]{5,0,4,3,2,1:T(8,128)S(1)} %collective-permute-done.2) | copy-start | bytes 884740
  125.9 8.6 %collective-permute-start.5 = (f32[32,3,2,3,6,1]{0,2,5,4,3,1:T(2,128)}, f32[32,3,2,3,6,1]{0,2,5,4,3,1:T(2,128)}, u32[]{:S(2)}, u32[]{:S(2)}) collective-permute-start(f32[32,3,2,3,6,1]{0,2,5,4,3,1:T(2,128)} %copy.507), channel_id=1, source_target_pairs={{1,0},{2,1},{3,2},{4,3},{5,4},{6,5},{7,6},{0,7},{9,8},{10,9},{11,1... | collective-permute-start | bytes 41480 | tf_op jit(solution)/shard_map/ppermute | solution.py:18
  132.8 9.4 %collective-permute-start.4 = (f32[32,3,2,3,6,1]{0,2,5,4,3,1:T(2,128)}, f32[32,3,2,3,6,1]{0,2,5,4,3,1:T(2,128)}, u32[]{:S(2)}, u32[]{:S(2)}) collective-permute-start(f32[32,3,2,3,6,1]{0,2,5,4,3,1:T(2,128)} %copy.506), channel_id=1, source_target_pairs={{0,1},{1,2},{2,3},{3,4},{4,5},{5,6},{6,7},{7,0},{8,9},{9,10},{10,1... | collective-permute-start | bytes 41480 | tf_op jit(solution)/shard_map/ppermute | solution.py:15
  143.8 1.4 copy-start.54
  143.8 1.5 copy-start.72
  143.8 1.5 copy-start.9
  143.8 1.5 copy-start.11
  145.4 1.5 copy-start
  147.9 1.1 copy-start.27
  147.9 1.2 copy-start.28
  147.9 1.2 copy-start.33
  148.6 1.1 copy-start.24
  148.6 1.2 copy-start.34
  304.4 133.4 %copy-start.94 = (f32[32,32]{1,0:T(8,128)}, f32[32,32]{1,0:T(8,128)S(1)}, u32[]{:S(2)}) copy-start(f32[32,32]{1,0:T(8,128)S(1)} %get-tuple-element.76) | copy-start | bytes 12292
  307.1 2.1 copy-start.37
  307.1 2.1 copy-start.93
  307.6 2.5 copy-start.2
  307.6 2.5 copy-start.39
  307.6 2.5 copy-start.91
  307.9 5.9 %collective-permute-start.6 = (f32[32,3,2,1,4,128]{5,0,4,3,2,1:T(8,128)S(1)}, f32[32,3,2,1,4,128]{5,0,4,3,2,1:T(8,128)S(1)}, u32[]{:S(2)}, u32[]{:S(2)}) collective-permute-start(f32[32,3,2,1,4,128]{5,0,4,3,2,1:T(8,128)S(1)} %copy.482), channel_id=1, source_target_pairs={{0,32},{32,64},{64,96},{96,128},{128,160},{160,192},{192,224},{224... | collective-permute-start | bytes 1179656 | tf_op jit(solution)/shard_map/ppermute | solution.py:15
  309.1 7.5 %collective-permute-start.7 = (f32[32,3,2,1,4,128]{5,0,4,3,2,1:T(8,128)S(1)}, f32[32,3,2,1,4,128]{5,0,4,3,2,1:T(8,128)S(1)}, u32[]{:S(2)}, u32[]{:S(2)}) collective-permute-start(f32[32,3,2,1,4,128]{5,0,4,3,2,1:T(8,128)S(1)} %copy.482), channel_id=1, source_target_pairs={{32,0},{64,32},{96,64},{128,96},{160,128},{192,160},{224,192},{0,2... | collective-permute-start | bytes 1179656 | tf_op jit(solution)/shard_map/ppermute | solution.py:18
  314.0 6.2 %copy-start.85 = (f32[3,3,4,128]{3,2,0,1:T(4,128)S(1)}, f32[3,3,4,128]{3,2,0,1:T(4,128)}, u32[]{:S(2)}) copy-start(f32[3,3,4,128]{3,2,0,1:T(4,128)} %copy-done.84) | copy-start | bytes 55300
  316.7 4.2 copy-start.83
  316.7 4.2 copy-start.89
  316.7 5.1 copy-start.81
  316.7 5.1 copy-start.87
  316.7 10.0 %collective-permute-start.8 = (f32[32,3,2,3,1,128]{5,0,4,3,2,1:T(8,128)S(1)}, f32[32,3,2,3,1,128]{5,0,4,3,2,1:T(8,128)S(1)}, u32[]{:S(2)}, u32[]{:S(2)}) collective-permute-start(f32[32,3,2,3,1,128]{5,0,4,3,2,1:T(8,128)S(1)} %get-tuple-element.113), channel_id=1, source_target_pairs={{0,8},{8,16},{16,24},{24,0},{1,9},{9,17},{17,25},{25,1},{2,10},{10... | collective-permute-start | bytes 884744 | tf_op jit(solution)/shard_map/ppermute | solution.py:15
  317.7 14.3 %collective-permute-start.9 = (f32[32,3,2,3,1,128]{5,0,4,3,2,1:T(8,128)S(1)}, f32[32,3,2,3,1,128]{5,0,4,3,2,1:T(8,128)S(1)}, u32[]{:S(2)}, u32[]{:S(2)}) collective-permute-start(f32[32,3,2,3,1,128]{5,0,4,3,2,1:T(8,128)S(1)} %get-tuple-element.114), channel_id=1, source_target_pairs={{8,0},{16,8},{24,16},{0,24},{9,1},{17,9},{25,17},{1,25},{10,2},{18... | collective-permute-start | bytes 884744 | tf_op jit(solution)/shard_map/ppermute | solution.py:18
  326.7 5.3 %copy-start.4 = (f32[32,3,2,3,1,128]{5,0,4,3,2,1:T(8,128)}, f32[32,3,2,3,1,128]{5,0,4,3,2,1:T(8,128)S(1)}, u32[]{:S(2)}) copy-start(f32[32,3,2,3,1,128]{5,0,4,3,2,1:T(8,128)S(1)} %collective-permute-done.8) | copy-start | bytes 884740
  337.6 8.1 %collective-permute-start.11 = (f32[32,3,2,3,6,1]{0,2,5,4,3,1:T(2,128)}, f32[32,3,2,3,6,1]{0,2,5,4,3,1:T(2,128)}, u32[]{:S(2)}, u32[]{:S(2)}) collective-permute-start(f32[32,3,2,3,6,1]{0,2,5,4,3,1:T(2,128)} %copy.509), channel_id=1, source_target_pairs={{1,0},{2,1},{3,2},{4,3},{5,4},{6,5},{7,6},{0,7},{9,8},{10,9},{11,1... | collective-permute-start | bytes 41480 | tf_op jit(solution)/shard_map/ppermute | solution.py:18
  345.0 9.9 %collective-permute-start.10 = (f32[32,3,2,3,6,1]{0,2,5,4,3,1:T(2,128)}, f32[32,3,2,3,6,1]{0,2,5,4,3,1:T(2,128)}, u32[]{:S(2)}, u32[]{:S(2)}) collective-permute-start(f32[32,3,2,3,6,1]{0,2,5,4,3,1:T(2,128)} %copy.508), channel_id=1, source_target_pairs={{0,1},{1,2},{2,3},{3,4},{4,5},{5,6},{6,7},{7,0},{8,9},{9,10},{10,1... | collective-permute-start | bytes 41480 | tf_op jit(solution)/shard_map/ppermute | solution.py:15
  347.2 2.2 copy-start.1
  347.2 2.2 copy-start.59
  347.2 2.2 copy-start.63
  356.4 1.4 copy-start.65
  356.5 1.5 copy-start.79
  356.5 1.6 copy-start.55
  356.5 1.6 copy-start.73
  356.5 1.7 copy-start.57
  356.5 1.7 copy-start.77
  359.3 1.1 copy-start.53
  359.9 1.1 copy-start.25
  359.9 1.2 copy-start.26
  359.9 1.2 copy-start.30
  359.9 1.3 copy-start.31
  360.6 1.1 copy-start.21
  360.6 1.2 copy-start.22
  360.6 1.2 copy-start.29
  360.6 1.3 copy-start.32
  (44 other events, 39.3 us)
where the time goes:
time: 524 us; the launch traced here: 522 us
  blocking collectives  377 us (72%)
  other arithmetic  45.5 us (9%)
  local copies, waits for them, and re-layouts  39 us (7%)
  waiting for transfers between devices  31.8 us (6%)
  starting transfers between devices  19.9 us (4%)
  matrix products  7.11 us (1%)
    psum x2, blocking collectives, lanczos_step(): alpha = lax.psum(local_gram(image, basis), ('gx', 'gy', 'gz')) / row_count  148 us
    psum x2, blocking collectives, lanczos_step(): lax.psum(local_gram(residual, residual), ('gx', 'gy', 'gz')) / row_count  147 us
    psum x1, blocking collectives, local(): lax.psum(local_gram(start_block, start_block), ('gx', 'gy', 'gz'))  81.5 us
    unnamed x203, local copies, waits for them, and re-layouts  17 us
    ppermute x6, waiting for transfers between devices, extended(): lax.ppermute(lax.slice_in_dim(block, block.shape[dim] - width, None, axis...  17 us
    ppermute x6, starting transfers between devices, extended(): lax.ppermute(lax.slice_in_dim(block, 0, width, axis=dim), axis, backward)  16.3 us
    ppermute x6, waiting for transfers between devices, extended(): lax.ppermute(lax.slice_in_dim(block, 0, width, axis=dim), axis, backward)  14.8 us
    reduce_sum x42, other arithmetic, apply_hessian(): summed = summed + jnp.sum(coupling[None] * neighbour[:, None], axis=2)  12.5 us
  transfers between devices with their start and end apart: 12, of which 8 were waited for; matrix products, arithmetic and copies ran while one was open for 6% of the time, Pallas kernels for 0%

commit v1 on v0

--- a/solution.py
+++ b/solution.py
@@ -4,6 +4,11 @@
 from jax.sharding import PartitionSpec as P
 
 PRECISE = lax.Precision.HIGHEST
+
+
+def one_after_other(value, first, second):
+    inner = lax.psum(value, first)
+    return lax.psum(inner, second)
 
 
 def extended(block, sides, width):
@@ -111,7 +116,9 @@
     row_count = start_block[0].size * device_count
     blocks = offset_blocks(pair_blocks, slot_map)
     onsite = onsite_blocks(blocks)
-    start_gram = lax.psum(local_gram(start_block, start_block), ("gx", "gy", "gz")) / row_count
+    start_gram = (
+        one_after_other(local_gram(start_block, start_block), "gx", ("gy", "gz")) / row_count
+    )
     lower0, inverse0 = inverse_factor(start_gram)
     basis1 = combine(inverse0, start_block)
     image1 = apply_hessian(basis1, blocks, onsite)

time: 524 us -> 640 us (1.22)
  blocking collectives: 377 us -> 464 us
  starting transfers between devices: 19.9 us -> 52 us
    psum x1 -> x2, blocking collectives: 81.5 us -> 168 us  [the longest x1 144 us: one_after_other(): return lax.psum(inner, second)]
    ppermute x6, starting transfers between devices: 3.56 us -> 43.7 us  [extended(): lax.ppermute(lax.slice_in_dim(block, block.shape[dim] - width, None, axis...]
    ppermute x6, starting transfers between devices: 16.3 us -> 8.29 us  [extended(): lax.ppermute(lax.slice_in_dim(block, 0, width, axis=dim), axis, backward)]
    ppermute x6, waiting for transfers between devices: 17 us -> 9.86 us  [extended(): lax.ppermute(lax.slice_in_dim(block, block.shape[dim] - width, None, axis...]
  transfers between devices with their start and end apart: 12 -> 12, of which waited for: 8 -> 8; matrix products, arithmetic and copies ran while one was open for 6% -> 5% of each run, Pallas kernels for 0% -> 0%
where the time goes in v1:
time: 640 us; the launch traced here: 639 us
  blocking collectives  464 us (72%)
  starting transfers between devices  52 us (8%)
  other arithmetic  45.5 us (7%)
  local copies, waits for them, and re-layouts  39 us (6%)
  waiting for transfers between devices  28.9 us (5%)
  matrix products  7.11 us (1%)
    psum x2, blocking collectives, lanczos_step(): alpha = lax.psum(local_gram(image, basis), ('gx', 'gy', 'gz')) / row_count  149 us
    psum x2, blocking collectives, lanczos_step(): lax.psum(local_gram(residual, residual), ('gx', 'gy', 'gz')) / row_count  147 us
    psum x1, blocking collectives, one_after_other(): return lax.psum(inner, second)  144 us
    ppermute x6, starting transfers between devices, extended(): lax.ppermute(lax.slice_in_dim(block, block.shape[dim] - width, None, axis...  43.7 us
    psum x1, blocking collectives, one_after_other(): inner = lax.psum(value, first)  23.7 us
    ppermute x6, waiting for transfers between devices, extended(): lax.ppermute(lax.slice_in_dim(block, 0, width, axis=dim), axis, backward)  19 us
    unnamed x203, local copies, waits for them, and re-layouts  17 us
  transfers between devices with their start and end apart: 12, of which 8 were waited for; matrix products, arithmetic and copies ran while one was open for 5% of the time, Pallas kernels for 0%

profile of v1, /device:TPU:1, one launch (start us, length us, event | category | flops | bytes accessed | tf_op | source)
XLA Modules:
  0.0 638.7 jit_solution(18299998534936220854)
XLA Ops:
  0.6 1.2 reshape.1549
  1.8 1.6 convolution_bitcast_fusion.2
  3.4 23.7 %psum.42 = f32[32,32]{0,1:T(8,128)S(1)} all-reduce(f32[32,32]{0,1:T(8,128)S(1)} %convolution_bitcast_fusion.2), channel_id=1, replica_groups=mesh['gx'=8,'gy'=4,'gz'=8] {'gx'}, use_global_device_ids=true, to_apply=%region_1.2 | all-reduce | flops 1024 | bytes 8192 | tf_op jit(solution)/shard_map/psum | solution.py:10
  27.1 144.3 %psum.43 = f32[32,32]{0,1:T(8,128)S(1)} all-reduce(f32[32,32]{0,1:T(8,128)S(1)} %psum.42), channel_id=1, replica_groups=mesh['gx'=8,'gy'=4,'gz'=8] {'gy','gz'}, use_global_device_ids=true, to_apply=%region_2.3 | all-reduce | flops 1024 | bytes 8192 | tf_op jit(solution)/shard_map/psum | solution.py:11
  171.5 2.9 cholesky.59
  175.1 0.7 fusion.44
  175.8 2.4 custom-call.7
  179.3 29.6 %collective-permute-start = (f32[32,3,2,1,4,128]{5,0,4,3,2,1:T(8,128)S(1)}, f32[32,3,2,1,4,128]{5,0,4,3,2,1:T(8,128)S(1)}, u32[]{:S(2)}, u32[]{:S(2)}) collective-permute-start(f32[32,3,2,1,4,128]{5,0,4,3,2,1:T(8,128)S(1)} %copy.391), channel_id=1, source_target_pairs={{0,32},{32,64},{64,96},{96,128},{128,160},{160,192},{192,224},{224... | collective-permute-start | bytes 1179656 | tf_op jit(solution)/shard_map/ppermute | solution.py:20
  208.8 1.9 collective-permute-start.1
  211.1 2.5 select_reduce_fusion.13
  220.8 0.8 multiply_reduce_fusion.45
  221.6 0.8 multiply_reduce_fusion.59
  222.7 4.8 collective-permute-start.2
  227.5 1.0 collective-permute-start.3
  228.5 0.7 slice_bitcast_fusion.9
  229.3 0.7 multiply_reduce_fusion.50
  230.0 0.9 multiply_reduce_fusion.55
  230.8 0.9 multiply_reduce_fusion.51
  231.7 1.0 collective-permute-done.2
  232.7 9.0 %collective-permute-done.3 = f32[32,3,2,3,1,128]{5,0,4,3,2,1:T(8,128)S(1)} collective-permute-done((f32[32,3,2,3,1,128]{5,0,4,3,2,1:T(8,128)S(1)}, f32[32,3,2,3,1,128]{5,0,4,3,2,1:T(8,128)S(1)}, u32[]{:S(2)}, u32[]{:S(2)}) %collective-permute-start.3) | collective-permute-done | bytes 294944 | tf_op jit(solution)/shard_map/ppermute | solution.py:23
  241.7 0.7 copy-done.10
  242.6 1.8 fusion.52
  244.5 2.8 copy.507
  247.9 1.3 copy.506
  249.2 4.7 collective-permute-start.4
  253.9 1.7 multiply_reduce_fusion.36
  255.6 2.7 copy.419
  258.3 0.9 collective-permute-done.4
  259.2 1.5 copy.395
  260.8 1.4 fusion.8
  268.0 74.9 %psum.44 = f32[32,32]{0,1:T(8,128)S(1)} all-reduce(f32[32,32]{0,1:T(8,128)S(1)} %fusion.56), channel_id=1, replica_groups=mesh['gx'=8,'gy'=4,'gz'=8] {'gx','gy','gz'}, use_global_device_ids=true, to_apply=%region_48.51 | all-reduce | flops 1024 | bytes 8192 | tf_op jit(solution)/shard_map/psum | solution.py:106
  343.9 73.4 %psum.45 = f32[32,32]{0,1:T(8,128)S(1)} all-reduce(f32[32,32]{0,1:T(8,128)S(1)} %fusion.57), channel_id=1, replica_groups=mesh['gx'=8,'gy'=4,'gz'=8] {'gx','gy','gz'}, use_global_device_ids=true, to_apply=%region_49.52 | all-reduce | flops 1024 | bytes 8192 | tf_op jit(solution)/shard_map/psum | solution.py:110
  417.4 2.9 cholesky.70
  421.6 2.4 custom-call.8
  425.9 0.8 multiply_reduce_fusion.15
  426.8 0.8 multiply_reduce_fusion.29
  428.3 2.1 collective-permute-done.6
  430.6 2.7 collective-permute-done.7
  433.4 1.7 collective-permute-start.8
  435.0 1.6 collective-permute-start.9
  436.8 0.7 multiply_reduce_fusion.20
  437.5 0.9 multiply_reduce_fusion.25
  438.4 0.9 multiply_reduce_fusion.21
  439.2 3.5 collective-permute-done.8
  442.7 7.3 %collective-permute-done.9 = f32[32,3,2,3,1,128]{5,0,4,3,2,1:T(8,128)S(1)} collective-permute-done((f32[32,3,2,3,1,128]{5,0,4,3,2,1:T(8,128)S(1)}, f32[32,3,2,3,1,128]{5,0,4,3,2,1:T(8,128)S(1)}, u32[]{:S(2)}, u32[]{:S(2)}) %collective-permute-start.9) | collective-permute-done | bytes 294944 | tf_op jit(solution)/shard_map/ppermute | solution.py:23
  450.1 0.7 copy-done.6
  451.0 1.8 fusion.51
  452.8 2.8 copy.509
  455.6 3.1 collective-permute-start.11
  458.7 1.5 multiply_reduce_fusion.6
  460.1 1.3 copy.508
  461.5 2.3 collective-permute-start.10
  463.8 1.5 copy.488
  465.3 2.2 maximum_bitcast_fusion.4
  467.6 0.9 multiply_reduce_fusion.17
  468.4 2.4 collective-permute-done.10
  470.8 1.5 copy.486
  472.4 1.4 fusion.4
  479.5 74.4 %psum.46 = f32[32,32]{0,1:T(8,128)S(1)} all-reduce(f32[32,32]{0,1:T(8,128)S(1)} %fusion.59), channel_id=1, replica_groups=mesh['gx'=8,'gy'=4,'gz'=8] {'gx','gy','gz'}, use_global_device_ids=true, to_apply=%region_80.83 | all-reduce | flops 1024 | bytes 8192 | tf_op jit(solution)/shard_map/psum | solution.py:106
  555.7 73.3 %psum.47 = f32[32,32]{0,1:T(8,128)S(1)} all-reduce(f32[32,32]{0,1:T(8,128)S(1)} %fusion.60), channel_id=1, replica_groups=mesh['gx'=8,'gy'=4,'gz'=8] {'gx','gy','gz'}, use_global_device_ids=true, to_apply=%region_81.84 | all-reduce | flops 1024 | bytes 8192 | tf_op jit(solution)/shard_map/psum | solution.py:110
  629.0 2.9 cholesky.81
  632.6 1.3 select_bitcast_fusion
  633.9 2.4 custom-call.9
  637.0 1.0 copy.497
  (322 shorter events, 30.2 us)
Async XLA Ops:
  3.4 207.3 %copy-start.95 = (s32[16,2,1,4,128]{4,3,2,1,0:T(4,128)S(1)}, s32[16,2,1,4,128]{4,3,2,1,0:T(4,128)}, u32[]{:S(2)}) copy-start(s32[16,2,1,4,128]{4,3,2,1,0:T(4,128)} %param.8) | copy-start | bytes 196612
  175.1 35.9 %copy-start.35 = (f32[3,3,16,2,1,4,128]{6,5,4,3,2,1,0:T(4,128)S(1)}, f32[3,3,16,2,1,4,128]{6,5,4,3,2,1,0:T(4,128)}, u32[]{:S(2)}) copy-start(f32[3,3,16,2,1,4,128]{6,5,4,3,2,1,0:T(4,128)} %param.7) | copy-start | bytes 1769476
  179.3 43.2 %collective-permute-start = (f32[32,3,2,1,4,128]{5,0,4,3,2,1:T(8,128)S(1)}, f32[32,3,2,1,4,128]{5,0,4,3,2,1:T(8,128)S(1)}, u32[]{:S(2)}, u32[]{:S(2)}) collective-permute-start(f32[32,3,2,1,4,128]{5,0,4,3,2,1:T(8,128)S(1)} %copy.391), channel_id=1, source_target_pairs={{0,32},{32,64},{64,96},{96,128},{128,160},{160,192},{192,224},{224... | collective-permute-start | bytes 1179656 | tf_op jit(solution)/shard_map/ppermute | solution.py:20
  208.8 13.8 %collective-permute-start.1 = (f32[32,3,2,1,4,128]{5,0,4,3,2,1:T(8,128)S(1)}, f32[32,3,2,1,4,128]{5,0,4,3,2,1:T(8,128)S(1)}, u32[]{:S(2)}, u32[]{:S(2)}) collective-permute-start(f32[32,3,2,1,4,128]{5,0,4,3,2,1:T(8,128)S(1)} %copy.391), channel_id=1, source_target_pairs={{32,0},{64,32},{96,64},{128,96},{160,128},{192,160},{224,192},{0,2... | collective-permute-start | bytes 1179656 | tf_op jit(solution)/shard_map/ppermute | solution.py:23
  216.8 12.4 %copy-start.84 = (f32[3,3,4,128]{3,2,0,1:T(4,128)}, f32[3,3,4,128]{3,2,0,1:T(4,128)S(1)}, u32[]{:S(2)}) copy-start(f32[3,3,4,128]{3,2,0,1:T(4,128)S(1)} %get-tuple-element.159) | copy-start | bytes 55300
  216.8 13.1 %copy-start.82 = (f32[3,3,4,128]{3,2,0,1:T(4,128)}, f32[3,3,4,128]{3,2,0,1:T(4,128)S(1)}, u32[]{:S(2)}) copy-start(f32[3,3,4,128]{3,2,0,1:T(4,128)S(1)} %get-tuple-element.162) | copy-start | bytes 55300
  217.5 13.4 %copy-start.80 = (f32[3,3,4,128]{3,2,0,1:T(4,128)}, f32[3,3,4,128]{3,2,0,1:T(4,128)S(1)}, u32[]{:S(2)}) copy-start(f32[3,3,4,128]{3,2,0,1:T(4,128)S(1)} %get-tuple-element.194) | copy-start | bytes 55300
  219.4 10.6 %copy-start.88 = (f32[3,3,4,128]{3,2,0,1:T(4,128)}, f32[3,3,4,128]{3,2,0,1:T(4,128)S(1)}, u32[]{:S(2)}) copy-start(f32[3,3,4,128]{3,2,0,1:T(4,128)S(1)} %get-tuple-element.190) | copy-start | bytes 55300
  219.4 11.4 %copy-start.86 = (f32[3,3,4,128]{3,2,0,1:T(4,128)}, f32[3,3,4,128]{3,2,0,1:T(4,128)S(1)}, u32[]{:S(2)}) copy-start(f32[3,3,4,128]{3,2,0,1:T(4,128)S(1)} %get-tuple-element.189) | copy-start | bytes 55300
  220.7 1.8 copy-start.90
  220.7 1.8 copy-start.92
  220.8 1.9 copy-start.36
  221.6 1.1 copy-start.38
  222.7 10.0 %collective-permute-start.2 = (f32[32,3,2,3,1,128]{5,0,4,3,2,1:T(8,128)S(1)}, f32[32,3,2,3,1,128]{5,0,4,3,2,1:T(8,128)S(1)}, u32[]{:S(2)}, u32[]{:S(2)}) collective-permute-start(f32[32,3,2,3,1,128]{5,0,4,3,2,1:T(8,128)S(1)} %get-tuple-element.115), channel_id=1, source_target_pairs={{0,8},{8,16},{16,24},{24,0},{1,9},{9,17},{17,25},{25,1},{2,10},{10... | collective-permute-start | bytes 884744 | tf_op jit(solution)/shard_map/ppermute | solution.py:20
  227.5 14.2 %collective-permute-start.3 = (f32[32,3,2,3,1,128]{5,0,4,3,2,1:T(8,128)S(1)}, f32[32,3,2,3,1,128]{5,0,4,3,2,1:T(8,128)S(1)}, u32[]{:S(2)}, u32[]{:S(2)}) collective-permute-start(f32[32,3,2,3,1,128]{5,0,4,3,2,1:T(8,128)S(1)} %get-tuple-element.116), channel_id=1, source_target_pairs={{8,0},{16,8},{24,16},{0,24},{9,1},{17,9},{25,17},{1,25},{10,2},{18... | collective-permute-start | bytes 884744 | tf_op jit(solution)/shard_map/ppermute | solution.py:23
  232.7 9.0 %copy-start.8 = (f32[32,3,2,3,1,128]{5,0,4,3,2,1:T(8,128)}, f32[32,3,2,3,1,128]{5,0,4,3,2,1:T(8,128)S(1)}, u32[]{:S(2)}) copy-start(f32[32,3,2,3,1,128]{5,0,4,3,2,1:T(8,128)S(1)} %collective-permute-done.2) | copy-start | bytes 884740
  247.3 8.3 %collective-permute-start.5 = (f32[32,3,2,3,6,1]{0,2,5,4,3,1:T(2,128)}, f32[32,3,2,3,6,1]{0,2,5,4,3,1:T(2,128)}, u32[]{:S(2)}, u32[]{:S(2)}) collective-permute-start(f32[32,3,2,3,6,1]{0,2,5,4,3,1:T(2,128)} %copy.507), channel_id=1, source_target_pairs={{1,0},{2,1},{3,2},{4,3},{5,4},{6,5},{7,6},{0,7},{9,8},{10,9},{11,1... | collective-permute-start | bytes 41480 | tf_op jit(solution)/shard_map/ppermute | solution.py:23
  249.2 10.0 %collective-permute-start.4 = (f32[32,3,2,3,6,1]{0,2,5,4,3,1:T(2,128)}, f32[32,3,2,3,6,1]{0,2,5,4,3,1:T(2,128)}, u32[]{:S(2)}, u32[]{:S(2)}) collective-permute-start(f32[32,3,2,3,6,1]{0,2,5,4,3,1:T(2,128)} %copy.506), channel_id=1, source_target_pairs={{0,1},{1,2},{2,3},{3,4},{4,5},{5,6},{6,7},{7,0},{8,9},{9,10},{10,1... | collective-permute-start | bytes 41480 | tf_op jit(solution)/shard_map/ppermute | solution.py:20
  260.8 1.4 copy-start.54
  260.8 1.5 copy-start.72
  260.8 1.5 copy-start.9
  260.8 1.5 copy-start.11
  262.4 1.5 copy-start
  264.9 1.1 copy-start.27
  264.9 1.2 copy-start.28
  264.9 1.2 copy-start.33
  265.6 1.1 copy-start.24
  265.6 1.2 copy-start.34
  421.6 132.9 %copy-start.94 = (f32[32,32]{1,0:T(8,128)}, f32[32,32]{1,0:T(8,128)S(1)}, u32[]{:S(2)}) copy-start(f32[32,32]{1,0:T(8,128)S(1)} %get-tuple-element.76) | copy-start | bytes 12292
  424.3 1.6 copy-start.37
  424.3 1.6 copy-start.93
  424.8 2.0 copy-start.2
  424.8 2.0 copy-start.39
  424.8 2.0 copy-start.91
  425.1 5.3 collective-permute-start.6
  425.7 7.5 %collective-permute-start.7 = (f32[32,3,2,1,4,128]{5,0,4,3,2,1:T(8,128)S(1)}, f32[32,3,2,1,4,128]{5,0,4,3,2,1:T(8,128)S(1)}, u32[]{:S(2)}, u32[]{:S(2)}) collective-permute-start(f32[32,3,2,1,4,128]{5,0,4,3,2,1:T(8,128)S(1)} %copy.482), channel_id=1, source_target_pairs={{32,0},{64,32},{96,64},{128,96},{160,128},{192,160},{224,192},{0,2... | collective-permute-start | bytes 1179656 | tf_op jit(solution)/shard_map/ppermute | solution.py:23
  430.6 6.2 copy-start.85
  433.3 4.2 copy-start.83
  433.3 4.2 copy-start.89
  433.3 5.1 copy-start.81
  433.3 5.1 copy-start.87
  433.4 9.4 %collective-permute-start.8 = (f32[32,3,2,3,1,128]{5,0,4,3,2,1:T(8,128)S(1)}, f32[32,3,2,3,1,128]{5,0,4,3,2,1:T(8,128)S(1)}, u32[]{:S(2)}, u32[]{:S(2)}) collective-permute-start(f32[32,3,2,3,1,128]{5,0,4,3,2,1:T(8,128)S(1)} %get-tuple-element.113), channel_id=1, source_target_pairs={{0,8},{8,16},{16,24},{24,0},{1,9},{9,17},{17,25},{25,1},{2,10},{10... | collective-permute-start | bytes 884744 | tf_op jit(solution)/shard_map/ppermute | solution.py:20
  435.0 15.0 %collective-permute-start.9 = (f32[32,3,2,3,1,128]{5,0,4,3,2,1:T(8,128)S(1)}, f32[32,3,2,3,1,128]{5,0,4,3,2,1:T(8,128)S(1)}, u32[]{:S(2)}, u32[]{:S(2)}) collective-permute-start(f32[32,3,2,3,1,128]{5,0,4,3,2,1:T(8,128)S(1)} %get-tuple-element.114), channel_id=1, source_target_pairs={{8,0},{16,8},{24,16},{0,24},{9,1},{17,9},{25,17},{1,25},{10,2},{18... | collective-permute-start | bytes 884744 | tf_op jit(solution)/shard_map/ppermute | solution.py:23
  442.7 7.3 %copy-start.4 = (f32[32,3,2,3,1,128]{5,0,4,3,2,1:T(8,128)}, f32[32,3,2,3,1,128]{5,0,4,3,2,1:T(8,128)S(1)}, u32[]{:S(2)}) copy-start(f32[32,3,2,3,1,128]{5,0,4,3,2,1:T(8,128)S(1)} %collective-permute-done.8) | copy-start | bytes 884740
  455.6 8.1 %collective-permute-start.11 = (f32[32,3,2,3,6,1]{0,2,5,4,3,1:T(2,128)}, f32[32,3,2,3,6,1]{0,2,5,4,3,1:T(2,128)}, u32[]{:S(2)}, u32[]{:S(2)}) collective-permute-start(f32[32,3,2,3,6,1]{0,2,5,4,3,1:T(2,128)} %copy.509), channel_id=1, source_target_pairs={{1,0},{2,1},{3,2},{4,3},{5,4},{6,5},{7,6},{0,7},{9,8},{10,9},{11,1... | collective-permute-start | bytes 41480 | tf_op jit(solution)/shard_map/ppermute | solution.py:23
  461.5 9.3 %collective-permute-start.10 = (f32[32,3,2,3,6,1]{0,2,5,4,3,1:T(2,128)}, f32[32,3,2,3,6,1]{0,2,5,4,3,1:T(2,128)}, u32[]{:S(2)}, u32[]{:S(2)}) collective-permute-start(f32[32,3,2,3,6,1]{0,2,5,4,3,1:T(2,128)} %copy.508), channel_id=1, source_target_pairs={{0,1},{1,2},{2,3},{3,4},{4,5},{5,6},{6,7},{7,0},{8,9},{9,10},{10,1... | collective-permute-start | bytes 41480 | tf_op jit(solution)/shard_map/ppermute | solution.py:20
  465.3 2.2 copy-start.1
  465.3 2.2 copy-start.59
  465.3 2.2 copy-start.63
  472.3 1.4 copy-start.65
  472.3 1.5 copy-start.79
  472.3 1.6 copy-start.55
  472.3 1.6 copy-start.73
  472.3 1.7 copy-start.57
  472.4 1.7 copy-start.77
  475.2 1.1 copy-start.53
  475.7 1.1 copy-start.25
  475.7 1.2 copy-start.26
  475.7 1.2 copy-start.30
  475.8 1.3 copy-start.31
  476.4 1.1 copy-start.21
  476.4 1.2 copy-start.22
  476.4 1.2 copy-start.29
  476.5 1.3 copy-start.32
  (44 other events, 39.3 us)
